TPU v7x, 512 devices: a whole 4x4x16 slice. The times are simulated.
512 devices in a mesh: lat: 16 (over z_hi, y, core), lon: 32 (over x, z_lo).
Axes of the slice: x: 4, y: 4, z: 16 (z_hi: 2, z_lo: 8; z = z_hi * 8 + z_lo), core: 2. Of those that a mesh axis runs over, the one named last changes fastest.
Arguments:
- bands: bfloat16 [16, 256, 320, 512], P('lat', 'lon'), may hold values from -6 to 6
- avail: int32 [16, 256, 10], P('lat', 'lon'), may hold values from 0 to 1, as said below
- latent_query: bfloat16 [4, 512], replicated, may hold values from -3 to 3
- w_band: bfloat16 [512, 1024], replicated, may hold values from -3.0935922 to 3.0935922
- w_mix: bfloat16 [512, 1536], replicated, may hold values from -3 to 3
- w_out: bfloat16 [512, 512], replicated, may hold values from -0.19921875 to 0.19921875
- offsets: int32 [5, 2], replicated, may hold values from -1 to 1, as said below
Outputs:
- encoded: bfloat16 [16, 256, 4, 512], P('lat', 'lon')
Inputs may be any that keep to these rules, and one draw needn't show every extreme that they name: `avail`: each patch has at least one available block. `offsets`: row 0 is (0, 0), rows 1 and 2 are (0, -1) and (0, 1), row 3 has latitude offset -1 and row 4 latitude offset +1; all rows differ.
All inputs are finite; a program needn't handle non-finite values.
Results may differ from a plain program's by a relative error of at most 0.03.
The roundings to bfloat16 on the way count: a program that leaves them out, or rounds other values in their place, can miss the bound.
Values may be sent and summed in bfloat16 or wider, within the bound.
No kernel may reach another device: no remote copies, remote signals or barrier semaphores. Data moves between devices by JAX's collectives and lax.ppermute only.
A program may use at most 64 MiB of HBM per device.

v0:
```python
import jax
import jax.numpy as jnp
from jax import lax
from jax.sharding import PartitionSpec as P

D = 512
HEADS = 16
HEAD = 32
BANDS = 320
BLOCK = 32
LATENTS = 4
NOFF = 5
EPS = 1e-06
NEG = -1e30


def padded(cells, sides, width):
    for axis, dim in sides:
        count = lax.axis_size(axis)
        head = lax.slice_in_dim(cells, 0, width, axis=dim)
        tail = lax.slice_in_dim(cells, cells.shape[dim] - width, cells.shape[dim], axis=dim)
        cells = jnp.concatenate(
            [
                lax.ppermute(tail, axis, [(i, (i + 1) % count) for i in range(count)]),
                cells,
                lax.ppermute(head, axis, [((i + 1) % count, i) for i in range(count)]),
            ],
            axis=dim,
        )
    return cells


def rms_rows(values):
    values = values.astype(jnp.float32)
    return values * lax.rsqrt(jnp.mean(values * values, axis=-1, keepdims=True) + EPS)


def softmax_weights(scores):
    peak_value = jnp.max(scores, axis=-1, keepdims=True)
    exponent = jnp.exp(scores - peak_value)
    return (exponent / jnp.sum(exponent, axis=-1, keepdims=True)).astype(jnp.bfloat16)


def per_device(bands, avail, latent_query, w_band, w_mix, w_out, offsets):
    columns = bands.shape[1]
    groups = HEADS // 2
    half_width = D // 2
    score_scale = HEAD ** (-0.5)
    normed = rms_rows(bands[0]).astype(jnp.bfloat16)
    key_value = jnp.dot(normed.reshape(-1, D), w_band, preferred_element_type=jnp.float32).astype(
        jnp.bfloat16
    )
    key_value = key_value.reshape(columns, BANDS, 2, HEADS, HEAD)
    queries = latent_query.reshape(LATENTS, HEADS, HEAD)
    scores = (
        jnp.einsum(
            "lhe,pbhe->plhb", queries, key_value[:, :, 0], preferred_element_type=jnp.float32
        )
        * score_scale
    )
    open_band = jnp.repeat(avail[0], BLOCK, axis=-1) > 0
    scores = jnp.where(open_band[:, None, None, :], scores, NEG)
    weights = softmax_weights(scores)
    pooled = jnp.einsum(
        "plhb,pbhe->plhe", weights, key_value[:, :, 1], preferred_element_type=jnp.float32
    )
    latent = pooled.reshape(columns, LATENTS, D) + latent_query.astype(jnp.float32)
    normal = rms_rows(latent)[None]
    mixture = jnp.dot(
        normal.astype(jnp.bfloat16).reshape(-1, D), w_mix, preferred_element_type=jnp.float32
    ).astype(jnp.bfloat16)
    mixture = mixture.reshape(1, columns, LATENTS, 3 * D)
    lat_queries = mixture[..., :D].reshape(1, columns, LATENTS, HEADS, HEAD)
    near_pairs = mixture[..., D : 2 * D]
    zonal_pairs = mixture[..., 2 * D :]
    framed = padded(near_pairs, (("lat", 0), ("lon", 1)), 1)
    zonal_row = lax.all_gather(zonal_pairs, "lon", axis=1, tiled=True)
    lat_index = lax.axis_index("lat")
    lat_count = lax.axis_size("lat")
    zero_index = jnp.zeros((), jnp.int32)
    near_keys = []
    near_open = []
    for offset_slot in range(NOFF):
        step_lat = offsets[offset_slot, 0]
        step_lon = offsets[offset_slot, 1]
        shifted = lax.dynamic_slice(
            framed, (1 + step_lat, 1 + step_lon, zero_index, zero_index), (1, columns, LATENTS, D)
        )
        near_keys.append(shifted)
        target = lat_index + step_lat
        near_open.append((target >= 0) & (target < lat_count))
    near_keys = jnp.stack(near_keys, axis=2).reshape(1, columns, NOFF * LATENTS, 2, groups, HEAD)
    open_keys = jnp.repeat(jnp.stack(near_open), LATENTS)
    scores = (
        jnp.einsum(
            "ijqhe,ijkhe->ijhqk",
            lat_queries[..., :groups, :],
            near_keys[..., 0, :, :],
            preferred_element_type=jnp.float32,
        )
        * score_scale
    )
    scores = jnp.where(open_keys, scores, NEG)
    weights = softmax_weights(scores)
    near_out = jnp.einsum(
        "ijhqk,ijkhe->ijqhe", weights, near_keys[..., 1, :, :], preferred_element_type=jnp.float32
    )
    row_keys = zonal_row.reshape(1, -1, 2, groups, HEAD)
    scores = (
        jnp.einsum(
            "ijqhe,ikhe->ijhqk",
            lat_queries[..., groups:, :],
            row_keys[:, :, 0],
            preferred_element_type=jnp.float32,
        )
        * score_scale
    )
    weights = softmax_weights(scores)
    zonal_out = jnp.einsum(
        "ijhqk,ikhe->ijqhe", weights, row_keys[:, :, 1], preferred_element_type=jnp.float32
    )
    attended = jnp.concatenate(
        [
            near_out.reshape(1, columns, LATENTS, half_width),
            zonal_out.reshape(1, columns, LATENTS, half_width),
        ],
        axis=-1,
    ).astype(jnp.bfloat16)
    update = jnp.dot(attended.reshape(-1, D), w_out, preferred_element_type=jnp.float32).reshape(
        1, columns, LATENTS, D
    )
    return (normal + update).astype(jnp.bfloat16)


def solution(mesh):
    return jax.shard_map(
        per_device,
        mesh=mesh,
        in_specs=(P("lat", "lon", None, None), P("lat", "lon", None), P(), P(), P(), P(), P()),
        out_specs=P("lat", "lon", None, None),
        check_vma=False,
    )
```

profile of v0, /device:TPU:8, one launch (start us, length us, event | category | flops | bytes accessed | tf_op | source)
XLA Modules:
  0.0 315.5 jit_solution(1022444642513698989)
XLA Ops:
  6.5 0.9 reshape.192
  7.4 0.8 add.179
  8.2 2.3 multiply_reduce_fusion
  10.6 2.4 fusion.2
  13.0 4.7 %convolution_convert_fusion = bf16[2560,1024]{1,0:T(8,128)(2,1)} fusion(bf16[2560,512]{1,0:T(8,128)(2,1)S(1)} %fusion.2, bf16[512,1024]{1,0:T(8,128)(2,1)S(1)} %copy-done.5), kind=kOutput, calls=%fused_computation.2 | convolution fusion | flops 2686976000 | bytes 8912896 | tf_op jit(solution)/shard_map/dot_general | solution.py:50
  17.7 7.7 %copy.58 = bf16[2560,1024]{0,1:T(8,128)(2,1)} copy(bf16[2560,1024]{1,0:T(8,128)(2,1)} %convolution_convert_fusion) | data formatting | bytes 10485760 | tf_op jit(solution)/shard_map/convert_element_type | solution.py:50
  25.4 10.9 %reshape.191 = bf16[8,320,2,16,32]{1,0,4,3,2:T(8,128)(2,1)} reshape(bf16[2560,1024]{0,1:T(8,128)(2,1)} %copy.58) | data formatting | bytes 10485760 | tf_op jit(solution)/shard_map/reshape | solution.py:53
  36.2 6.5 %fusion.32 = (bf16[8,320,1,16,32]{1,0,4,3,2:T(8,128)(2,1)}, bf16[8,320,1,16,32]{1,0,4,3,2:T(8,128)(2,1)}) fusion(bf16[8,320,2,16,32]{1,0,4,3,2:T(8,128)(2,1)} %reshape.191), kind=kLoop, calls=%fused_computation.65 | loop fusion | bytes 10485760 | tf_op jit(solution)/shard_map/slice | solution.py:57
  43.0 2.8 fusion.39
  45.8 3.3 %multiply_reduce_fusion.1 = (f32[8,4]{1,0:T(8,128)S(1)}, f32[8,4,16,32]{3,1,2,0:T(4,128)S(1)}) fusion(f32[4,16,32]{2,0,1:T(4,128)S(1)} %copy.64, bf16[8,320,1,16,32]{1,0,4,3,2:T(8,128)(2,1)} %get-tuple-element.6, f32[8,4,16,320]{3,1,0,2:T(4,128)S(1)} %get-tuple-element.28, f32[8,4,16]{1,0,2:T(8,128)S(1)} %get-tuple-element.27), kind=kOutput, calls=%fused_computation.41 | convolution fusion | flops 10862560 | bytes 3352704 | tf_op jit(solution)/shard_map/plhb,pbhe->plhe/dot_general | solution.py:64
  49.4 0.4 convolution_convert_fusion.1
  49.9 1.9 collective-permute-start
  51.8 3.6 %collective-permute-start.1 = (bf16[1,8,4,512]{3,1,2,0:T(8,128)(2,1)S(1)}, bf16[1,8,4,512]{3,1,2,0:T(8,128)(2,1)S(1)}, u32[]{:S(2)}, u32[]{:S(2)}) collective-permute-start(bf16[1,8,4,512]{3,1,2,0:T(8,128)(2,1)S(1)} %copy.87), channel_id=1, source_target_pairs={{32,0},{64,32},{96,64},{128,96},{160,128},{192,160},{224,192},{256... | collective-permute-start | bytes 98312 | tf_op jit(solution)/shard_map/ppermute | solution.py:26
  55.5 0.6 slice.101
  56.4 0.7 collective-permute-done.1
  57.1 3.8 %collective-permute-start.2 = (bf16[3,1,4,512]{3,1,2,0:T(2,128)(2,1)S(1)}, bf16[3,1,4,512]{3,1,2,0:T(2,128)(2,1)S(1)}, u32[]{:S(2)}, u32[]{:S(2)}) collective-permute-start(bf16[3,1,4,512]{3,1,2,0:T(2,128)(2,1)S(1)} %get-tuple-element.13), channel_id=1, source_target_pairs={{0,1},{1,2},{2,3},{3,4},{4,5},{5,6},{6,7},{7,8},{8,9},{9,10},{10,1... | collective-permute-start | bytes 36872 | tf_op jit(solution)/shard_map/ppermute | solution.py:24
  60.9 13.6 %collective-permute-start.3 = (bf16[3,1,4,512]{3,1,2,0:T(2,128)(2,1)S(1)}, bf16[3,1,4,512]{3,1,2,0:T(2,128)(2,1)S(1)}, u32[]{:S(2)}, u32[]{:S(2)}) collective-permute-start(bf16[3,1,4,512]{3,1,2,0:T(2,128)(2,1)S(1)} %get-tuple-element.14), channel_id=1, source_target_pairs={{1,0},{2,1},{3,2},{4,3},{5,4},{6,5},{7,6},{8,7},{9,8},{10,9},{11,1... | collective-permute-start | bytes 36872 | tf_op jit(solution)/shard_map/ppermute | solution.py:26
  74.6 0.7 fusion.38
  91.8 0.3 reshape.196
  92.3 0.5 fusion.41
  92.8 0.3 fusion.16
  93.3 197.7 %all-gather.2.cloned.1.call-done = bf16[1,256,4,512]{3,2,0,1:T(4,128)(2,1)} async-done(((bf16[1,8,4,512]{3,2,0,1:T(4,128)(2,1)}), bf16[1,256,4,512]{3,2,0,1:T(4,128)(2,1)}) %all-gather.2.cloned.1.call-update) | async-done | bytes 1048592 | tf_op jit(solution)/shard_map/all_gather | solution.py:77
  291.0 6.0 %reshape.202 = bf16[1,1024,2,8,32]{4,3,2,1,0:T(8,128)(2,1)} reshape(bf16[1,256,4,512]{3,2,0,1:T(4,128)(2,1)} %all-gather.2.cloned.1.call-done) | data formatting | bytes 2097152 | tf_op jit(solution)/shard_map/reshape | solution.py:108
  297.0 4.5 %fusion.33 = (bf16[1,1024,1,8,32]{4,3,2,1,0:T(8,128)(2,1)}, bf16[1,1024,1,8,32]{4,3,2,1,0:T(8,128)(2,1)}) fusion(bf16[1,1024,2,8,32]{4,3,2,1,0:T(8,128)(2,1)} %reshape.202), kind=kLoop, calls=%fused_computation.66 | loop fusion | bytes 2097152 | tf_op jit(solution)/shard_map/slice | solution.py:113
  301.5 2.5 copy.93
  304.0 2.5 copy.92
  306.4 0.4 fusion.40
  306.8 0.3 fusion.19
  307.1 0.4 fusion.15
  307.6 0.2 copy-done.1
  307.9 0.2 fusion.18
  308.1 0.6 copy.79
  (56 shorter events, 2.1 us)
Async XLA Ops:
  6.5 42.8 %copy-start = (bf16[512,1536]{1,0:T(8,128)(2,1)S(1)}, bf16[512,1536]{1,0:T(8,128)(2,1)}, u32[]{:S(2)}) copy-start(bf16[512,1536]{1,0:T(8,128)(2,1)} %param.11) | copy-start | bytes 4718596
  6.5 284.5 %all-gather.2.cloned.1.call-start = ((), (), s32[]{:S(2)}) async-start(), calls=%async_computation | async-start | bytes 1081344 | tf_op jit(solution)/shard_map/all_gather | solution.py:77
  10.5 2.5 copy-start.5
  36.2 6.5 %copy-start.4 = (s32[1,8,10]{2,1,0:T(8,128)S(1)}, s32[1,8,10]{2,1,0:T(8,128)}, u32[]{:S(2)}) copy-start(s32[1,8,10]{2,1,0:T(8,128)} %param.8) | copy-start | bytes 964
  45.8 3.5 %copy-start.2 = (bf16[4,512]{1,0:T(4,128)(2,1)S(1)}, bf16[4,512]{1,0:T(4,128)(2,1)}, u32[]{:S(2)}) copy-start(bf16[4,512]{1,0:T(4,128)(2,1)} %param.9) | copy-start | bytes 12292
  49.1 25.5 %copy-start.3 = (s32[5,2]{0,1:T(2,128)S(1)}, s32[5,2]{0,1:T(2,128)}, u32[]{:S(2)}) copy-start(s32[5,2]{0,1:T(2,128)} %param.13) | copy-start | bytes 124
  49.9 6.4 %collective-permute-start = (bf16[1,8,4,512]{3,1,2,0:T(8,128)(2,1)S(1)}, bf16[1,8,4,512]{3,1,2,0:T(8,128)(2,1)S(1)}, u32[]{:S(2)}, u32[]{:S(2)}) collective-permute-start(bf16[1,8,4,512]{3,1,2,0:T(8,128)(2,1)S(1)} %copy.87), channel_id=1, source_target_pairs={{0,32},{32,64},{64,96},{96,128},{128,160},{160,192},{192,224},{224... | collective-permute-start | bytes 98312 | tf_op jit(solution)/shard_map/ppermute | solution.py:24
  51.8 5.2 %collective-permute-start.1 = (bf16[1,8,4,512]{3,1,2,0:T(8,128)(2,1)S(1)}, bf16[1,8,4,512]{3,1,2,0:T(8,128)(2,1)S(1)}, u32[]{:S(2)}, u32[]{:S(2)}) collective-permute-start(bf16[1,8,4,512]{3,1,2,0:T(8,128)(2,1)S(1)} %copy.87), channel_id=1, source_target_pairs={{32,0},{64,32},{96,64},{128,96},{160,128},{192,160},{224,192},{256... | collective-permute-start | bytes 98312 | tf_op jit(solution)/shard_map/ppermute | solution.py:26
  57.1 34.4 %collective-permute-start.2 = (bf16[3,1,4,512]{3,1,2,0:T(2,128)(2,1)S(1)}, bf16[3,1,4,512]{3,1,2,0:T(2,128)(2,1)S(1)}, u32[]{:S(2)}, u32[]{:S(2)}) collective-permute-start(bf16[3,1,4,512]{3,1,2,0:T(2,128)(2,1)S(1)} %get-tuple-element.13), channel_id=1, source_target_pairs={{0,1},{1,2},{2,3},{3,4},{4,5},{5,6},{6,7},{7,8},{8,9},{9,10},{10,1... | collective-permute-start | bytes 36872 | tf_op jit(solution)/shard_map/ppermute | solution.py:24
  60.9 30.6 %collective-permute-start.3 = (bf16[3,1,4,512]{3,1,2,0:T(2,128)(2,1)S(1)}, bf16[3,1,4,512]{3,1,2,0:T(2,128)(2,1)S(1)}, u32[]{:S(2)}, u32[]{:S(2)}) collective-permute-start(bf16[3,1,4,512]{3,1,2,0:T(2,128)(2,1)S(1)} %get-tuple-element.14), channel_id=1, source_target_pairs={{1,0},{2,1},{3,2},{4,3},{5,4},{6,5},{7,6},{8,7},{9,8},{10,9},{11,1... | collective-permute-start | bytes 36872 | tf_op jit(solution)/shard_map/ppermute | solution.py:26
  306.8 1.0 copy-start.1
Sparse Core Ops, SparseCore 0:
  56.2 234.7 all-gather.1
where the time goes:
time: 317 us; the launch traced here: 316 us
  waiting for transfers between devices  198 us (62%)
  local copies, waits for them, and re-layouts  46.6 us (15%)
  between operations  29.4 us (9%)
  starting transfers between devices  23 us (7%)
  matrix products  13 us (4%)
  other arithmetic  5.12 us (2%)
    all_gather x1, waiting for transfers between devices, per_device(): zonal_row = lax.all_gather(zonal_pairs, 'lon', axis=1, tiled=True)  198 us
    ppermute x2, starting transfers between devices, padded(): lax.ppermute(head, axis, [((i + 1) % count, i) for i in range(count)])  17.3 us
    reshape x1, local copies, waits for them, and re-layouts, per_device(): key_value = key_value.reshape(columns, BANDS, 2, HEADS, HEAD)  10.9 us
    convert_element_type x1, local copies, waits for them, and re-layouts, per_device(): jnp.dot(normed.reshape(-1, D), w_band, preferred_element_type=jnp.float32)  7.68 us
    slice x1, local copies, waits for them, and re-layouts, per_device(): key_value[:, :, 0]  6.54 us
  transfers between devices with their start and end apart: 5, of which 2 were waited for; matrix products, arithmetic and copies ran while one was open for 1% of the time, Pallas kernels for 0%

commit v1 on v0

--- a/solution.py
+++ b/solution.py
@@ -74,7 +74,10 @@
     near_pairs = mixture[..., D : 2 * D]
     zonal_pairs = mixture[..., 2 * D :]
     framed = padded(near_pairs, (("lat", 0), ("lon", 1)), 1)
-    zonal_row = lax.all_gather(zonal_pairs, "lon", axis=1, tiled=True)
+    size = lax.axis_size("lon")
+    blocks = jnp.stack([zonal_pairs for _ in range(size)])
+    blocks = lax.all_to_all(blocks, "lon", split_axis=0, concat_axis=0)
+    zonal_row = jnp.concatenate(blocks, axis=1)
     lat_index = lax.axis_index("lat")
     lat_count = lax.axis_size("lat")
     zero_index = jnp.zeros((), jnp.int32)

time: 317 us -> 160 us (0.50)
  the two profiles are of different devices: /device:TPU:8 before, /device:TPU:66 now
where the time goes in v1:
time: 160 us; the launch traced here: 159 us
  local copies, waits for them, and re-layouts  49.8 us (31%)
  starting transfers between devices  37.2 us (23%)
  waiting for transfers between devices  36.3 us (23%)
  between operations  15.9 us (10%)
  matrix products  14.9 us (9%)
  other arithmetic  5.16 us (3%)
    ppermute x2, waiting for transfers between devices, padded(): lax.ppermute(tail, axis, [(i, (i + 1) % count) for i in range(count)])  36.3 us
    ppermute x2, starting transfers between devices, padded(): lax.ppermute(head, axis, [((i + 1) % count, i) for i in range(count)])  18.6 us
    all_to_all x1, starting transfers between devices, per_device(): blocks = lax.all_to_all(blocks, 'lon', split_axis=0, concat_axis=0)  14.8 us
    reshape x1, local copies, waits for them, and re-layouts, per_device(): key_value = key_value.reshape(columns, BANDS, 2, HEADS, HEAD)  10.9 us
    unnamed x19, local copies, waits for them, and re-layouts  7.71 us
    convert_element_type x1, local copies, waits for them, and re-layouts, per_device(): jnp.dot(normed.reshape(-1, D), w_band, preferred_element_type=jnp.float32)  7.68 us
    slice x1, local copies, waits for them, and re-layouts, per_device(): key_value[:, :, 0]  6.54 us
    dot_general x1, matrix products, per_device(): jnp.dot(normed.reshape(-1, D), w_band, preferred_element_type=jnp.float32)  4.66 us
  transfers between devices with their start and end apart: 5, of which 1 were waited for; matrix products, arithmetic and copies ran while one was open for 6% of the time, Pallas kernels for 0%

profile of v1, /device:TPU:66, one launch (start us, length us, event | category | flops | bytes accessed | tf_op | source)
XLA Modules:
  0.0 159.2 jit_solution(5573635578674334126)
XLA Ops:
  0.0 0.9 reshape.192
  0.9 0.8 add.179
  1.7 2.3 %multiply_reduce_fusion = f32[8,320]{1,0:T(8,128)S(1)} fusion(bf16[1,8,320,512]{3,2,1,0:T(8,128)(2,1)} %param.7), kind=kLoop, calls=%fused_computation.5 | loop fusion | flops 3929600 | bytes 2631680 | tf_op jit(solution)/shard_map/reduce_sum | solution.py:35
  4.1 2.4 %fusion.2 = bf16[2560,512]{1,0:T(8,128)(2,1)S(1)} fusion(f32[2560]{0:T(1024)S(1)} %rsqrt.24, bf16[1,8,320,512]{3,2,1,0:T(8,128)(2,1)} %param.7), kind=kLoop, calls=%fused_computation.4 | loop fusion | flops 3932160 | bytes 5253120 | tf_op jit(solution)/shard_map/convert_element_type | solution.py:49
  6.5 4.7 %convolution_convert_fusion = bf16[2560,1024]{1,0:T(8,128)(2,1)} fusion(bf16[2560,512]{1,0:T(8,128)(2,1)S(1)} %fusion.2, bf16[512,1024]{1,0:T(8,128)(2,1)S(1)} %copy-done.5), kind=kOutput, calls=%fused_computation.2 | convolution fusion | flops 2686976000 | bytes 8912896 | tf_op jit(solution)/shard_map/dot_general | solution.py:50
  11.1 7.7 %copy.42 = bf16[2560,1024]{0,1:T(8,128)(2,1)} copy(bf16[2560,1024]{1,0:T(8,128)(2,1)} %convolution_convert_fusion) | data formatting | bytes 10485760 | tf_op jit(solution)/shard_map/convert_element_type | solution.py:50
  18.8 10.9 %reshape.191 = bf16[8,320,2,16,32]{1,0,4,3,2:T(8,128)(2,1)} reshape(bf16[2560,1024]{0,1:T(8,128)(2,1)} %copy.42) | data formatting | bytes 10485760 | tf_op jit(solution)/shard_map/reshape | solution.py:53
  29.7 6.5 %fusion.32 = (bf16[8,320,1,16,32]{1,0,4,3,2:T(8,128)(2,1)}, bf16[8,320,1,16,32]{1,0,4,3,2:T(8,128)(2,1)}) fusion(bf16[8,320,2,16,32]{1,0,4,3,2:T(8,128)(2,1)} %reshape.191), kind=kLoop, calls=%fused_computation.71 | loop fusion | bytes 10485760 | tf_op jit(solution)/shard_map/slice | solution.py:57
  36.4 2.8 %fusion.38 = (f32[8,4,16]{1,0,2:T(8,128)S(1)}, f32[8,4,16,320]{3,1,0,2:T(4,128)S(1)}) fusion(bf16[8,320,1,16,32]{1,0,4,3,2:T(8,128)(2,1)} %get-tuple-element.5, pred[8,320]{1,0:T(8,128)(4,1)S(1)} %gt.20, bf16[4,16,32,1]{2,1,0,3:T(8,128)(2,1)S(1)} %bitcast.144), kind=kOutput, calls=%fused_computation.77 | convolution fusion | flops 11141439 | bytes 3285504 | tf_op jit(solution)/shard_map/sub | solution.py:40
  39.3 3.2 %multiply_reduce_fusion.1 = (f32[8,4]{1,0:T(8,128)S(1)}, f32[8,4,16,32]{3,1,2,0:T(4,128)S(1)}) fusion(f32[4,16,32]{2,0,1:T(4,128)S(1)} %copy.48, bf16[8,320,1,16,32]{1,0,4,3,2:T(8,128)(2,1)} %get-tuple-element.6, f32[8,4,16,320]{3,1,0,2:T(4,128)S(1)} %get-tuple-element.34, f32[8,4,16]{1,0,2:T(8,128)S(1)} %get-tuple-element.33), kind=kOutput, calls=%fused_computation.41 | convolution fusion | flops 10862560 | bytes 3352704 | tf_op jit(solution)/shard_map/plhb,pbhe->plhe/dot_general | solution.py:64
  43.4 1.5 stack.38
  44.8 14.8 %all-to-all-start = ((bf16[32,1,8,4,512]{4,3,2,1,0:T(4,128)(2,1)}), bf16[32,1,8,4,512]{4,3,2,1,0:T(4,128)(2,1)S(1)}, u32[]{:S(2)}, u32[]{:S(2)}) async-start(bf16[32,1,8,4,512]{4,3,2,1,0:T(4,128)(2,1)} %stack.38), calls=%async_computation | async-start | bytes 2097152 | tf_op jit(solution)/shard_map/all_to_all | solution.py:79
  59.6 1.9 %collective-permute-start = (bf16[1,8,4,512]{3,2,1,0:T(4,128)(2,1)S(1)}, bf16[1,8,4,512]{3,2,1,0:T(4,128)(2,1)S(1)}, u32[]{:S(2)}, u32[]{:S(2)}) collective-permute-start(bf16[1,8,4,512]{3,2,1,0:T(4,128)(2,1)S(1)} %get-tuple-element.20), channel_id=1, source_target_pairs={{0,32},{32,64},{64,96},{96,128},{128,160},{160,192},{192,224},{224... | collective-permute-start | bytes 98312 | tf_op jit(solution)/shard_map/ppermute | solution.py:24
  61.5 14.5 %collective-permute-start.1 = (bf16[1,8,4,512]{3,2,1,0:T(4,128)(2,1)S(1)}, bf16[1,8,4,512]{3,2,1,0:T(4,128)(2,1)S(1)}, u32[]{:S(2)}, u32[]{:S(2)}) collective-permute-start(bf16[1,8,4,512]{3,2,1,0:T(4,128)(2,1)S(1)} %get-tuple-element.20), channel_id=1, source_target_pairs={{32,0},{64,32},{96,64},{128,96},{160,128},{192,160},{224,192},{256... | collective-permute-start | bytes 98312 | tf_op jit(solution)/shard_map/ppermute | solution.py:26
  76.2 36.3 %collective-permute-done = bf16[1,8,4,512]{3,2,1,0:T(4,128)(2,1)S(1)} collective-permute-done((bf16[1,8,4,512]{3,2,1,0:T(4,128)(2,1)S(1)}, bf16[1,8,4,512]{3,2,1,0:T(4,128)(2,1)S(1)}, u32[]{:S(2)}, u32[]{:S(2)}) %collective-permute-start) | collective-permute-done | bytes 32800 | tf_op jit(solution)/shard_map/ppermute | solution.py:24
  112.5 1.9 %collective-permute-start.2 = (bf16[3,1,4,512]{3,2,1,0:T(4,128)(2,1)S(1)}, bf16[3,1,4,512]{3,2,1,0:T(4,128)(2,1)S(1)}, u32[]{:S(2)}, u32[]{:S(2)}) collective-permute-start(bf16[3,1,4,512]{3,2,1,0:T(4,128)(2,1)S(1)} %get-tuple-element.18), channel_id=1, source_target_pairs={{0,1},{1,2},{2,3},{3,4},{4,5},{5,6},{6,7},{7,8},{8,9},{9,10},{10,1... | collective-permute-start | bytes 36872 | tf_op jit(solution)/shard_map/ppermute | solution.py:24
  114.5 4.1 %collective-permute-start.3 = (bf16[3,1,4,512]{3,2,1,0:T(4,128)(2,1)S(1)}, bf16[3,1,4,512]{3,2,1,0:T(4,128)(2,1)S(1)}, u32[]{:S(2)}, u32[]{:S(2)}) collective-permute-start(bf16[3,1,4,512]{3,2,1,0:T(4,128)(2,1)S(1)} %get-tuple-element.19), channel_id=1, source_target_pairs={{1,0},{2,1},{3,2},{4,3},{5,4},{6,5},{7,6},{8,7},{9,8},{10,9},{11,1... | collective-permute-start | bytes 36872 | tf_op jit(solution)/shard_map/ppermute | solution.py:26
  118.6 0.7 fusion.37
  135.6 0.6 bitcast_dynamic-update-slice_fusion.4
  136.2 0.6 bitcast_dynamic-update-slice_fusion.3
  136.8 0.6 bitcast_dynamic-update-slice_fusion.2
  137.5 0.6 bitcast_dynamic-update-slice_fusion.1
  138.1 0.6 bitcast_dynamic-update-slice_fusion
  138.7 1.3 reshape.196
  140.0 1.0 fusion.34
  141.1 1.5 fusion.40
  142.5 1.3 fusion.16
  144.0 3.6 %reshape_reshape.3 = bf16[1,1024,2,8,32]{4,3,2,1,0:T(8,128)(2,1)} reshape(bf16[32,1,8,4,512]{4,3,2,1,0:T(4,128)(2,1)S(1)} %all-to-all-done) | data formatting | bytes 2097152 | tf_op jit(solution)/shard_map/reshape;reshape | solution.py:111
  147.6 4.5 %fusion.33 = (bf16[1,1024,1,8,32]{4,3,2,1,0:T(8,128)(2,1)}, bf16[1,1024,1,8,32]{4,3,2,1,0:T(8,128)(2,1)}) fusion(bf16[1,1024,2,8,32]{4,3,2,1,0:T(8,128)(2,1)} %reshape_reshape.3), kind=kLoop, calls=%fused_computation.72 | loop fusion | bytes 2097152 | tf_op jit(solution)/shard_map/slice | solution.py:116
  152.0 2.5 %copy.79 = bf16[1,1024,1,8,32]{1,4,3,2,0:T(8,128)(2,1)S(1)} copy(bf16[1,1024,1,8,32]{4,3,2,1,0:T(8,128)(2,1)} %get-tuple-element.7) | data formatting | bytes 1048576
  154.5 2.5 %copy.78 = bf16[1,1024,1,8,32]{1,4,3,2,0:T(8,128)(2,1)S(1)} copy(bf16[1,1024,1,8,32]{4,3,2,1,0:T(8,128)(2,1)} %get-tuple-element.8) | data formatting | bytes 1048576
  158.6 0.6 copy.66
  (52 shorter events, 3.7 us)
Async XLA Ops:
  0.0 42.9 %copy-start = (bf16[512,1536]{1,0:T(8,128)(2,1)S(1)}, bf16[512,1536]{1,0:T(8,128)(2,1)}, u32[]{:S(2)}) copy-start(bf16[512,1536]{1,0:T(8,128)(2,1)} %param.11) | copy-start | bytes 4718596
  4.0 2.5 %copy-start.5 = (bf16[512,1024]{1,0:T(8,128)(2,1)S(1)}, bf16[512,1024]{1,0:T(8,128)(2,1)}, u32[]{:S(2)}) copy-start(bf16[512,1024]{1,0:T(8,128)(2,1)} %param.10) | copy-start | bytes 3145732
  29.7 6.5 %copy-start.4 = (s32[1,8,10]{2,1,0:T(8,128)S(1)}, s32[1,8,10]{2,1,0:T(8,128)}, u32[]{:S(2)}) copy-start(s32[1,8,10]{2,1,0:T(8,128)} %param.8) | copy-start | bytes 964
  39.3 3.5 %copy-start.2 = (bf16[4,512]{1,0:T(4,128)(2,1)S(1)}, bf16[4,512]{1,0:T(4,128)(2,1)}, u32[]{:S(2)}) copy-start(bf16[4,512]{1,0:T(4,128)(2,1)} %param.9) | copy-start | bytes 12292
  42.7 75.9 %copy-start.3 = (s32[5,2]{0,1:T(2,128)S(1)}, s32[5,2]{0,1:T(2,128)}, u32[]{:S(2)}) copy-start(s32[5,2]{0,1:T(2,128)} %param.13) | copy-start | bytes 124
  44.8 99.2 %all-to-all-start = ((bf16[32,1,8,4,512]{4,3,2,1,0:T(4,128)(2,1)}), bf16[32,1,8,4,512]{4,3,2,1,0:T(4,128)(2,1)S(1)}, u32[]{:S(2)}, u32[]{:S(2)}) async-start(bf16[32,1,8,4,512]{4,3,2,1,0:T(4,128)(2,1)} %stack.38), calls=%async_computation | async-start | bytes 2097152 | tf_op jit(solution)/shard_map/all_to_all | solution.py:79
  59.6 52.9 %collective-permute-start = (bf16[1,8,4,512]{3,2,1,0:T(4,128)(2,1)S(1)}, bf16[1,8,4,512]{3,2,1,0:T(4,128)(2,1)S(1)}, u32[]{:S(2)}, u32[]{:S(2)}) collective-permute-start(bf16[1,8,4,512]{3,2,1,0:T(4,128)(2,1)S(1)} %get-tuple-element.20), channel_id=1, source_target_pairs={{0,32},{32,64},{64,96},{96,128},{128,160},{160,192},{192,224},{224... | collective-permute-start | bytes 98312 | tf_op jit(solution)/shard_map/ppermute | solution.py:24
  61.5 51.0 %collective-permute-start.1 = (bf16[1,8,4,512]{3,2,1,0:T(4,128)(2,1)S(1)}, bf16[1,8,4,512]{3,2,1,0:T(4,128)(2,1)S(1)}, u32[]{:S(2)}, u32[]{:S(2)}) collective-permute-start(bf16[1,8,4,512]{3,2,1,0:T(4,128)(2,1)S(1)} %get-tuple-element.20), channel_id=1, source_target_pairs={{32,0},{64,32},{96,64},{128,96},{160,128},{192,160},{224,192},{256... | collective-permute-start | bytes 98312 | tf_op jit(solution)/shard_map/ppermute | solution.py:26
  112.5 22.8 %collective-permute-start.2 = (bf16[3,1,4,512]{3,2,1,0:T(4,128)(2,1)S(1)}, bf16[3,1,4,512]{3,2,1,0:T(4,128)(2,1)S(1)}, u32[]{:S(2)}, u32[]{:S(2)}) collective-permute-start(bf16[3,1,4,512]{3,2,1,0:T(4,128)(2,1)S(1)} %get-tuple-element.18), channel_id=1, source_target_pairs={{0,1},{1,2},{2,3},{3,4},{4,5},{5,6},{6,7},{7,8},{8,9},{9,10},{10,1... | collective-permute-start | bytes 36872 | tf_op jit(solution)/shard_map/ppermute | solution.py:24
  114.5 20.9 %collective-permute-start.3 = (bf16[3,1,4,512]{3,2,1,0:T(4,128)(2,1)S(1)}, bf16[3,1,4,512]{3,2,1,0:T(4,128)(2,1)S(1)}, u32[]{:S(2)}, u32[]{:S(2)}) collective-permute-start(bf16[3,1,4,512]{3,2,1,0:T(4,128)(2,1)S(1)} %get-tuple-element.19), channel_id=1, source_target_pairs={{1,0},{2,1},{3,2},{4,3},{5,4},{6,5},{7,6},{8,7},{9,8},{10,9},{11,1... | collective-permute-start | bytes 36872 | tf_op jit(solution)/shard_map/ppermute | solution.py:26
  157.3 1.0 copy-start.1
